TPU v7x, 32 devices: a whole 2x2x4 slice. The times are simulated.
32 devices in a mesh: grp: 4 (over y, x), sub: 8 (over z, core).
Axes of the slice: x: 2, y: 2, z: 4, core: 2. Of those that a mesh axis runs over, the one named last changes fastest.
Arguments:
- right_side: float32 [24576, 160], P(('grp', 'sub')), may hold values from -6 to 6
- iterate_in: float32 [24576, 160], P(('grp', 'sub')), may hold values from -6 to 6
- diagonal: float32 [24576], P(('grp', 'sub')), may hold values from 1.5 to 4
- block_values: bfloat16 [32, 6, 3, 128, 128], P(('grp', 'sub')), may hold values from -0.125 to 0.125
- block_cols: int32 [32, 6, 3], P(('grp', 'sub')), may hold values from 0 to 5, as said below
- couple_left: bfloat16 [24576, 128], P(('grp', 'sub')), may hold values from -0.125 to 0.125
- couple_right: bfloat16 [24576, 128], P(('grp', 'sub')), may hold values from -0.125 to 0.125
- send_rows: int32 [32, 2, 128], P(('grp', 'sub')), may hold values from 0 to 767, as said below
- local_inverse: bfloat16 [32, 1024, 1024], P(('grp', 'sub')), may hold values from -0.3 to 2.3, as said below
- coarse_basis: bfloat16 [32, 1024, 32], P(('grp', 'sub')), may hold values from -0.1875 to 0.1875
- coarse_diag: float32 [32, 32, 32], P(('grp', 'sub')), may hold values from -54 to 59.5, as said below
- coarse_up: float32 [32, 32, 32], P(('grp', 'sub')), may hold values from -29.7 to 27
Outputs:
- iterate: float32 [24576, 160], P(('grp', 'sub'))
- residual: float32 [24576, 160], P(('grp', 'sub'))
Inputs may be any that keep to these rules, and one draw needn't show every extreme that they name: `block_cols`: the 3 column blocks of one row block are distinct. `send_rows`: the 256 rows listed for one subdomain are distinct. `local_inverse`: each block is symmetric positive definite. `coarse_diag`: each block is symmetric; with coarse_up the coarse operator is symmetric positive definite.
All inputs are finite; a program needn't handle non-finite values.
Results may differ from a plain program's by a relative error of at most 0.0032.
Values may be sent and summed in bfloat16 or wider, within the bound.
No kernel may reach another device: no remote copies, remote signals or barrier semaphores. Data moves between devices by JAX's collectives and lax.ppermute only.
A program may use at most 64 MiB of HBM per device.

v0:
```python
import jax
import jax.numpy as jnp
from jax import lax
from jax.sharding import PartitionSpec as P


def with_halo(cells, sides, width):
    for axis, dim in sides:
        count = lax.axis_size(axis)
        ends = count - 1
        head = lax.slice_in_dim(cells, 0, width, axis=dim)
        tail = lax.slice_in_dim(cells, cells.shape[dim] - width, cells.shape[dim], axis=dim)
        cells = jnp.concatenate(
            [
                lax.ppermute(tail, axis, [(i, (i + 1) % count) for i in range(ends)]),
                cells,
                lax.ppermute(head, axis, [((i + 1) % count, i) for i in range(ends)]),
            ],
            axis=dim,
        )
    return cells


def chol_solve(factor, values):
    halfway = lax.linalg.triangular_solve(factor, values, left_side=True, lower=True)
    return lax.linalg.triangular_solve(
        factor, halfway, left_side=True, lower=True, transpose_a=True
    )


def solve_chain(diagonal_blocks, upper, values):
    highest = lax.Precision.HIGHEST
    blocks_total = diagonal_blocks.shape[0]
    padded_total = 1
    while padded_total < blocks_total:
        padded_total = padded_total * 2
    extra = padded_total - blocks_total
    block_width = diagonal_blocks.shape[1]
    identity = jnp.eye(block_width, dtype=jnp.float32)
    diag_now = jnp.concatenate(
        [diagonal_blocks, jnp.broadcast_to(identity, (extra, block_width, block_width))], axis=0
    )
    upper_now = jnp.concatenate(
        [upper[:-1], jnp.zeros((extra + 1, block_width, block_width), jnp.float32)], axis=0
    )
    rhs_now = jnp.concatenate([values, jnp.zeros((extra,) + values.shape[1:], jnp.float32)], axis=0)
    levels = []
    while diag_now.shape[0] > 1:
        diag_even = diag_now[0::2]
        diag_odd = diag_now[1::2]
        upper_even = upper_now[0::2]
        upper_odd = upper_now[1::2]
        rhs_even = rhs_now[0::2]
        rhs_odd = rhs_now[1::2]
        factor = jnp.linalg.cholesky(diag_odd)
        stacked = jnp.concatenate([jnp.swapaxes(upper_even, 1, 2), upper_odd, rhs_odd], axis=2)
        through = chol_solve(factor, stacked)
        toward_left = through[:, :, :block_width]
        toward_right = through[:, :, block_width : 2 * block_width]
        odd_loads = through[:, :, 2 * block_width :]
        new_diag = diag_even - jnp.einsum(
            "mab,mbc->mac", upper_even, toward_left, precision=highest
        )
        new_upper = -jnp.einsum("mab,mbc->mac", upper_even, toward_right, precision=highest)
        new_rhs = rhs_even - jnp.einsum("mab,mbn->man", upper_even, odd_loads, precision=highest)
        from_diag = jnp.einsum("mba,mbc->mac", upper_odd, toward_right, precision=highest)
        from_rhs = jnp.einsum("mba,mbn->man", upper_odd, odd_loads, precision=highest)
        new_diag = new_diag - jnp.concatenate(
            [jnp.zeros_like(from_diag[:1]), from_diag[:-1]], axis=0
        )
        new_rhs = new_rhs - jnp.concatenate([jnp.zeros_like(from_rhs[:1]), from_rhs[:-1]], axis=0)
        levels.append((toward_left, toward_right, odd_loads))
        diag_now, upper_now, rhs_now = (new_diag, new_upper, new_rhs)
    solution = chol_solve(jnp.linalg.cholesky(diag_now[0]), rhs_now[0])[None]
    for toward_left, toward_right, odd_loads in reversed(levels):
        next_sol = jnp.concatenate([solution[1:], jnp.zeros_like(solution[:1])], axis=0)
        odd_part = (
            odd_loads
            - jnp.einsum("mab,mbn->man", toward_left, solution, precision=highest)
            - jnp.einsum("mab,mbn->man", toward_right, next_sol, precision=highest)
        )
        solution = jnp.stack([solution, odd_part], axis=1).reshape((-1,) + solution.shape[1:])
    return solution[:blocks_total]


def shards(
    right_side,
    iterate_in,
    diagonal,
    block_values,
    block_cols,
    couple_left,
    couple_right,
    send_rows,
    local_inverse,
    coarse_basis,
    coarse_diag,
    coarse_up,
):
    bf16 = jnp.bfloat16
    f32 = jnp.float32
    highest = lax.Precision.HIGHEST
    intersection = send_rows.shape[2]
    rows_own = right_side.shape[0]
    cases = right_side.shape[1]
    row_blocks = block_cols.shape[1]
    modes = coarse_basis.shape[2]
    column_blocks = block_cols[0]
    sent_left_rows = send_rows[0, 0]
    sent_right_rows = send_rows[0, 1]

    def neighbour_rows(source):
        boundary = jnp.stack([source[sent_left_rows], source[sent_right_rows]])
        padded = with_halo(boundary, ((("grp", "sub"), 0),), 1)
        return (padded[0], padded[3])

    def apply_operator(vector):
        rounded = vector.astype(bf16)
        from_left, from_right = neighbour_rows(rounded)
        blocks = rounded.reshape(row_blocks, -1, cases)
        picked = blocks[column_blocks]
        sparse = jnp.einsum(
            "itab,itbn->ian", block_values[0], picked, preferred_element_type=f32
        ).reshape(rows_own, cases)
        coupled = jnp.dot(couple_left, from_left, preferred_element_type=f32) + jnp.dot(
            couple_right, from_right, preferred_element_type=f32
        )
        return diagonal[:, None] * vector + (sparse + coupled)

    residual_start = right_side - apply_operator(iterate_in)
    rounded = residual_start.astype(bf16)
    from_left, from_right = neighbour_rows(rounded)
    extended = jnp.concatenate([from_left, rounded, from_right], axis=0)
    local_part = jnp.dot(local_inverse[0], extended, preferred_element_type=f32)
    coarse_in = jnp.dot(coarse_basis[0].T, extended, preferred_element_type=f32)
    blocks_diag = lax.all_gather(coarse_diag, "sub", axis=0, tiled=True)
    blocks_up = lax.all_gather(coarse_up, "sub", axis=0, tiled=True)
    group = lax.axis_index("grp")
    groups = lax.axis_size("grp")
    member = lax.axis_index("sub")
    members = lax.axis_size("sub")
    keep = (group < groups - 1).astype(f32)
    first_up = blocks_up[0]
    last_up = blocks_up[members - 1] * keep
    columns = lax.all_gather(coarse_in[None], "sub", axis=0, tiled=True)
    width = columns.shape[2]
    inner_count = members - 1
    empty_cols = jnp.zeros((inner_count, modes, modes), f32)
    left_cols = empty_cols.at[0].set(first_up.T)
    right_cols = empty_cols.at[inner_count - 1].set(last_up)
    stacked = jnp.concatenate([columns[1:], left_cols, right_cols], axis=2)
    solved = solve_chain(blocks_diag[1:], blocks_up[1:], stacked)
    sol_loads = solved[:, :, :width]
    sol_left = solved[:, :, width : width + modes]
    sol_right = solved[:, :, width + modes :]
    self_left = jnp.dot(first_up, sol_left[0], precision=highest)
    cross_term = jnp.dot(first_up, sol_right[0], precision=highest)
    rhs_first = jnp.dot(first_up, sol_loads[0], precision=highest)
    self_right = jnp.dot(last_up.T, sol_right[-1], precision=highest)
    rhs_last = jnp.dot(last_up.T, sol_loads[-1], precision=highest)
    sep_diag = lax.all_gather(blocks_diag[0][None], "grp", axis=0, tiled=True)
    sep_rhs = lax.all_gather(columns[0][None], "grp", axis=0, tiled=True)
    all_left = lax.all_gather(self_left[None], "grp", axis=0, tiled=True)
    all_right = lax.all_gather(self_right[None], "grp", axis=0, tiled=True)
    all_cross = lax.all_gather(cross_term[None], "grp", axis=0, tiled=True)
    all_first = lax.all_gather(rhs_first[None], "grp", axis=0, tiled=True)
    all_last = lax.all_gather(rhs_last[None], "grp", axis=0, tiled=True)
    prev_right = jnp.concatenate([jnp.zeros_like(all_right[:1]), all_right[:-1]], axis=0)
    prev_last = jnp.concatenate([jnp.zeros_like(all_last[:1]), all_last[:-1]], axis=0)
    reduced_diag = sep_diag - all_left - prev_right
    reduced_rhs = sep_rhs - all_first - prev_last
    sep_sol = solve_chain(reduced_diag, -all_cross, reduced_rhs)
    padded_sol = jnp.concatenate([sep_sol, jnp.zeros_like(sep_sol[:1])], axis=0)
    mine = lax.dynamic_index_in_dim(padded_sol, group, 0, keepdims=False)
    after = lax.dynamic_index_in_dim(padded_sol, group + 1, 0, keepdims=False)
    inner_sol = (
        sol_loads
        - jnp.einsum("ivw,wn->ivn", sol_left, mine, precision=highest)
        - jnp.einsum("ivw,wn->ivn", sol_right, after, precision=highest)
    )
    group_sol = jnp.concatenate([mine[None], inner_sol], axis=0)
    coarse_sol = lax.dynamic_index_in_dim(group_sol, member, 0, keepdims=False)
    correction = local_part + jnp.dot(
        coarse_basis[0], coarse_sol.astype(bf16), preferred_element_type=f32
    )
    tails = jnp.stack([correction[:intersection], correction[intersection + rows_own :]])
    returned = with_halo(tails.astype(jnp.bfloat16), ((("grp", "sub"), 0),), 1).astype(tails.dtype)
    owned = correction[intersection : intersection + rows_own]
    owned = owned.at[sent_right_rows].add(returned[3])
    owned = owned.at[sent_left_rows].add(returned[0])
    inner = lax.psum(jnp.sum(residual_start * owned, axis=0), ("grp", "sub"))
    image = apply_operator(owned)
    curvature = lax.psum(jnp.sum(owned * image, axis=0), ("grp", "sub"))
    step_size = inner / curvature
    return (iterate_in + step_size * owned, residual_start - step_size * image)


def solution(mesh):
    in_specs = (
        P(("grp", "sub"), None),
        P(("grp", "sub"), None),
        P(("grp", "sub")),
        P(("grp", "sub"), None, None, None, None),
        P(("grp", "sub"), None, None),
        P(("grp", "sub"), None),
        P(("grp", "sub"), None),
        P(("grp", "sub"), None, None),
        P(("grp", "sub"), None, None),
        P(("grp", "sub"), None, None),
        P(("grp", "sub"), None, None),
        P(("grp", "sub"), None, None),
    )
    out_specs = (P(("grp", "sub"), None), P(("grp", "sub"), None))
    return jax.shard_map(shards, mesh=mesh, in_specs=in_specs, out_specs=out_specs, check_vma=False)
```

profile of v0, /device:TPU:14, one launch (start us, length us, event | category | flops | bytes accessed | tf_op | source)
XLA Modules:
  0.0 289.2 jit_solution(11546375033526299166)
XLA Ops:
  7.7 2.4 collective-permute-start
  10.4 14.8 %all_gather.32 = f32[8,32,32]{2,1,0:T(8,128)S(1)} all-gather(f32[1,32,32]{2,1,0:T(8,128)S(1)} %copy-done.34), channel_id=1, replica_groups=mesh['grp'=4,'sub'=8] {'sub'}, dimensions={0}, use_global_device_ids=true | all-gather | bytes 36864 | tf_op jit(solution)/shard_map/all_gather | solution.py:137
  25.2 14.0 %all_gather.30 = f32[8,32,32]{2,1,0:T(8,128)S(1)} all-gather(f32[1,32,32]{2,1,0:T(8,128)S(1)} %copy-done.35), channel_id=1, replica_groups=mesh['grp'=4,'sub'=8] {'sub'}, dimensions={0}, use_global_device_ids=true | all-gather | bytes 36864 | tf_op jit(solution)/shard_map/all_gather | solution.py:136
  39.5 11.7 %custom-call.47 = f32[4,32,32]{2,1,0:T(8,128)S(1)} custom-call(f32[4,32,32]{2,1,0:T(8,128)S(1)} %copy.185), custom_call_target="Cholesky" | custom-call | tf_op jit(solution)/shard_map/jit(cholesky)/cholesky | solution.py:55
  61.8 4.0 %collective-permute-start.3 = (bf16[1,128,160]{1,2,0:T(8,128)(2,1)S(1)}, bf16[1,128,160]{1,2,0:T(8,128)(2,1)S(1)}, u32[]{:S(2)}, u32[]{:S(2)}) collective-permute-start(bf16[1,128,160]{1,2,0:T(8,128)(2,1)S(1)} %bitcast.412), channel_id=1, source_target_pairs={{1,0},{2,1},{3,2},{4,3},{5,4},{6,5},{7,6},{8,7},{9,8},{10,9},{11,1... | collective-permute-start | bytes 122888 | tf_op jit(solution)/shard_map/ppermute | solution.py:17
  68.7 11.2 %custom-call.48 = f32[4,1,32,32]{2,3,1,0:T(8,128)} custom-call(f32[4,1,32,32]{3,2,1,0:T(8,128)} %select_bitcast_fusion), custom_call_target="InvertDiagBlocksLowerTriangular" | custom-call | tf_op jit(solution)/shard_map/triangular_solve | solution.py:26
  79.9 9.1 %all_gather.31 = f32[4,32,32]{2,1,0:T(8,128)S(1)} all-gather(f32[1,32,32]{2,1,0:T(8,128)S(1)} %slice-done.1), channel_id=1, replica_groups=mesh['grp'=4,'sub'=8] {'grp'}, dimensions={0}, use_global_device_ids=true | all-gather | bytes 20480 | tf_op jit(solution)/shard_map/all_gather | solution.py:161
  90.5 12.7 %all-gather = f32[256,160]{1,0:T(8,128)S(1)} all-gather(f32[32,160]{1,0:T(8,128)S(1)} %convolution_bitcast_fusion.11), channel_id=2, replica_groups=mesh['grp'=4,'sub'=8] {'sub'}, dimensions={0}, use_global_device_ids=true | all-gather | bytes 184320 | tf_op jit(solution)/shard_map/all_gather | solution.py:145
  106.0 5.9 %custom-call.57 = f32[2,32,32]{2,1,0:T(8,128)S(1)} custom-call(f32[2,32,32]{2,1,0:T(8,128)S(1)} %fusion.117), custom_call_target="Cholesky" | custom-call | tf_op jit(solution)/shard_map/jit(cholesky)/cholesky | solution.py:55
  112.1 4.9 %custom-call.49 = f32[2,1,32,32]{2,3,1,0:T(8,128)S(1)} custom-call(f32[2,1,32,32]{3,2,1,0:T(8,128)S(1)} %fusion.119), custom_call_target="InvertDiagBlocksLowerTriangular" | custom-call | tf_op jit(solution)/shard_map/triangular_solve | solution.py:26
  119.1 2.9 %custom-call.58 = f32[1,32,32]{2,1,0:T(8,128)S(1)} custom-call(f32[1,32,32]{2,1,0:T(8,128)S(1)} %fusion.169), custom_call_target="Cholesky" | custom-call | tf_op jit(solution)/shard_map/jit(cholesky)/cholesky | solution.py:55
  123.2 2.4 custom-call.50
  126.9 2.9 %cholesky.184 = f32[32,32]{1,0:T(8,128)S(1)} custom-call(f32[32,32]{1,0:T(8,128)S(1)} %fusion.150), custom_call_target="Cholesky" | custom-call | tf_op jit(solution)/shard_map/jit(cholesky)/cholesky | solution.py:74
  131.1 2.4 custom-call.51
  136.5 7.0 %all-gather.6 = f32[128,160]{1,0:T(8,128)S(1)} all-gather(f32[32,160]{1,0:T(8,128)S(1)} %slice-done), channel_id=8, replica_groups=mesh['grp'=4,'sub'=8] {'grp'}, dimensions={0}, use_global_device_ids=true | all-gather | bytes 102400 | tf_op jit(solution)/shard_map/all_gather | solution.py:162
  143.4 8.9 %all-gather.4 = f32[128,160]{1,0:T(8,128)S(1)} all-gather(f32[32,160]{1,0:T(8,128)S(1)} %convolution_bitcast_fusion.7), channel_id=6, replica_groups=mesh['grp'=4,'sub'=8] {'grp'}, dimensions={0}, use_global_device_ids=true | all-gather | bytes 102400 | tf_op jit(solution)/shard_map/all_gather | solution.py:166
  152.4 7.1 %all-gather.5 = f32[128,160]{1,0:T(8,128)S(1)} all-gather(f32[32,160]{1,0:T(8,128)S(1)} %fusion.101), channel_id=7, replica_groups=mesh['grp'=4,'sub'=8] {'grp'}, dimensions={0}, use_global_device_ids=true | all-gather | bytes 102400 | tf_op jit(solution)/shard_map/all_gather | solution.py:167
  159.6 8.7 %all-gather.3 = f32[128,32]{1,0:T(8,128)S(1)} all-gather(f32[32,32]{1,0:T(8,128)S(1)} %copy.214), channel_id=5, replica_groups=mesh['grp'=4,'sub'=8] {'grp'}, dimensions={0}, use_global_device_ids=true | all-gather | bytes 20480 | tf_op jit(solution)/shard_map/all_gather | solution.py:165
  168.5 6.7 %all-gather.2 = f32[128,32]{1,0:T(8,128)S(1)} all-gather(f32[32,32]{1,0:T(8,128)S(1)} %fusion.145), channel_id=4, replica_groups=mesh['grp'=4,'sub'=8] {'grp'}, dimensions={0}, use_global_device_ids=true | all-gather | bytes 20480 | tf_op jit(solution)/shard_map/all_gather | solution.py:164
  175.4 8.9 %all-gather.1 = f32[128,32]{1,0:T(8,128)S(1)} all-gather(f32[32,32]{1,0:T(8,128)S(1)} %copy.208), channel_id=3, replica_groups=mesh['grp'=4,'sub'=8] {'grp'}, dimensions={0}, use_global_device_ids=true | all-gather | bytes 20480 | tf_op jit(solution)/shard_map/all_gather | solution.py:163
  184.6 5.9 %custom-call.59 = f32[2,32,32]{2,1,0:T(8,128)S(1)} custom-call(f32[2,32,32]{2,1,0:T(8,128)S(1)} %fusion.112), custom_call_target="Cholesky" | custom-call | tf_op jit(solution)/shard_map/jit(cholesky)/cholesky | solution.py:55
  190.7 4.9 %custom-call.52 = f32[2,1,32,32]{2,3,1,0:T(8,128)S(1)} custom-call(f32[2,1,32,32]{3,2,1,0:T(8,128)S(1)} %fusion.118), custom_call_target="InvertDiagBlocksLowerTriangular" | custom-call | tf_op jit(solution)/shard_map/triangular_solve | solution.py:26
  197.6 2.9 %custom-call.60 = f32[1,32,32]{2,1,0:T(8,128)S(1)} custom-call(f32[1,32,32]{2,1,0:T(8,128)S(1)} %fusion.158), custom_call_target="Cholesky" | custom-call | tf_op jit(solution)/shard_map/jit(cholesky)/cholesky | solution.py:55
  201.9 2.4 custom-call.53
  205.5 2.9 %cholesky.216 = f32[32,32]{1,0:T(8,128)S(1)} custom-call(f32[32,32]{1,0:T(8,128)S(1)} %fusion.149), custom_call_target="Cholesky" | custom-call | tf_op jit(solution)/shard_map/jit(cholesky)/cholesky | solution.py:74
  209.8 2.4 custom-call.54
  217.3 2.4 collective-permute-start.4
  220.1 4.3 %collective-permute-done.4 = bf16[1,128,160]{1,2,0:T(8,128)(2,1)S(1)} collective-permute-done((bf16[1,128,160]{1,2,0:T(8,128)(2,1)S(1)}, bf16[1,128,160]{1,2,0:T(8,128)(2,1)S(1)}, u32[]{:S(2)}, u32[]{:S(2)}) %collective-permute-start.4) | collective-permute-done | bytes 40992 | tf_op jit(solution)/shard_map/ppermute | solution.py:15
  233.4 2.4 collective-permute-start.6
  238.6 3.1 %collective-permute-done.6 = bf16[1,128,160]{2,1,0:T(8,128)(2,1)S(1)} collective-permute-done((bf16[1,128,160]{2,1,0:T(8,128)(2,1)S(1)}, bf16[1,128,160]{2,1,0:T(8,128)(2,1)S(1)}, u32[]{:S(2)}, u32[]{:S(2)}) %collective-permute-start.6) | collective-permute-done | bytes 40992 | tf_op jit(solution)/shard_map/ppermute | solution.py:15
  242.8 44.1 %all-reduce.16 = (f32[160]{0:T(256)S(1)}, f32[160]{0:T(256)S(1)}) all-reduce(f32[160]{0:T(256)S(1)} %get-tuple-element.30, f32[160]{0:T(256)S(1)} %get-tuple-element.29), channel_id=1, replica_groups=mesh['grp'=4,'sub'=8] {'grp','sub'}, use_global_device_ids=true, to_apply=%region_11.15 | all-reduce | flops 320 | bytes 2560 | tf_op jit(solution)/shard_map/psum | solution.py:191
  286.9 2.3 multiply_subtract_fusion
  (282 shorter events, 58.2 us)
Async XLA Ops:
  0.6 213.9 %copy-start = (bf16[1,1024,1024]{2,1,0:T(8,128)(2,1)S(1)}, bf16[1,1024,1024]{2,1,0:T(8,128)(2,1)}, u32[]{:S(2)}) copy-start(bf16[1,1024,1024]{2,1,0:T(8,128)(2,1)} %param.27) | copy-start | bytes 6291460
  0.6 9.5 %copy-start.43 = (s32[1,6,3]{1,0,2:T(1,128)S(1)}, s32[1,6,3]{1,0,2:T(1,128)}, u32[]{:S(2)}) copy-start(s32[1,6,3]{1,0,2:T(1,128)} %param.23) | copy-start | bytes 220
  0.7 9.7 %copy-start.34 = (f32[1,32,32]{2,1,0:T(8,128)S(1)}, f32[1,32,32]{2,1,0:T(8,128)}, u32[]{:S(2)}) copy-start(f32[1,32,32]{2,1,0:T(8,128)} %param.30) | copy-start | bytes 12292
  0.7 24.5 %copy-start.35 = (f32[1,32,32]{2,1,0:T(8,128)S(1)}, f32[1,32,32]{2,1,0:T(8,128)}, u32[]{:S(2)}) copy-start(f32[1,32,32]{2,1,0:T(8,128)} %param.29) | copy-start | bytes 12292
  2.8 7.3 %copy-start.38 = (s32[128]{0:T(128)}, s32[128]{0:T(128)S(1)}, u32[]{:S(2)}) copy-start(s32[128]{0:T(128)S(1)} %get-tuple-element.52) | copy-start | bytes 1540
  2.8 22.4 %copy-start.40 = (s32[128]{0:T(128)}, s32[128]{0:T(128)S(1)}, u32[]{:S(2)}) copy-start(s32[128]{0:T(128)S(1)} %get-tuple-element.51) | copy-start | bytes 1540
  2.8 22.4 %copy-start.36 = (s32[1024]{0:T(1024)}, s32[1024]{0:T(1024)S(1)}, u32[]{:S(2)}) copy-start(s32[1024]{0:T(1024)S(1)} %get-tuple-element.59) | copy-start | bytes 12292
  2.8 22.4 %copy-start.37 = (s32[1024]{0:T(1024)}, s32[1024]{0:T(1024)S(1)}, u32[]{:S(2)}) copy-start(s32[1024]{0:T(1024)S(1)} %get-tuple-element.58) | copy-start | bytes 12292
  4.3 52.1 %collective-permute-start.1 = (bf16[1,128,160]{2,1,0:T(8,128)(2,1)}, bf16[1,128,160]{2,1,0:T(8,128)(2,1)}, u32[]{:S(2)}, u32[]{:S(2)}) collective-permute-start(bf16[1,128,160]{2,1,0:T(8,128)(2,1)} %bitcast.13), channel_id=1, source_target_pairs={{1,0},{2,1},{3,2},{4,3},{5,4},{6,5},{7,6},{8,7},{9,8},{10,9},{11,1... | collective-permute-start | bytes 122888 | tf_op jit(solution)/shard_map/ppermute | solution.py:17
  7.7 49.8 %collective-permute-start = (bf16[1,128,160]{2,1,0:T(8,128)(2,1)}, bf16[1,128,160]{2,1,0:T(8,128)(2,1)}, u32[]{:S(2)}, u32[]{:S(2)}) collective-permute-start(bf16[1,128,160]{2,1,0:T(8,128)(2,1)} %bitcast.9), channel_id=1, source_target_pairs={{0,1},{1,2},{2,3},{3,4},{4,5},{5,6},{6,7},{7,8},{8,9},{9,10},{10,1... | collective-permute-start | bytes 122888 | tf_op jit(solution)/shard_map/ppermute | solution.py:15
  10.1 43.6 %copy-start.24 = (pred[32,32]{1,0:T(8,128)(4,1)}, pred[32,32]{1,0:T(8,128)(4,1)S(1)}, u32[]{:S(2)}) copy-start(pred[32,32]{1,0:T(8,128)(4,1)S(1)} %iota_compare_fusion.3) | copy-start | bytes 3076
  10.2 45.5 %copy-start.22 = (pred[32,32]{1,0:T(8,128)(4,1)}, pred[32,32]{1,0:T(8,128)(4,1)S(1)}, u32[]{:S(2)}) copy-start(pred[32,32]{1,0:T(8,128)(4,1)S(1)} %iota_compare_fusion.7) | copy-start | bytes 3076
  10.4 43.3 %copy-start.30 = (s32[1024]{0:T(1024)}, s32[1024]{0:T(1024)S(1)}, u32[]{:S(2)}) copy-start(s32[1024]{0:T(1024)S(1)} %pad_clamp_fusion.2) | copy-start | bytes 12292
  39.2 12.7 %copy-start.11 = (f32[8,32,32]{2,1,0:T(8,128)}, f32[8,32,32]{2,1,0:T(8,128)S(1)}, u32[]{:S(2)}) copy-start(f32[8,32,32]{2,1,0:T(8,128)S(1)} %all_gather.30) | copy-start | bytes 98308
  56.4 46.9 %copy-start.13 = (f32[1,32,32]{2,1,0:T(8,128)}, f32[1,32,32]{2,1,0:T(8,128)S(1)}, u32[]{:S(2)}) copy-start(f32[1,32,32]{2,1,0:T(8,128)S(1)} %get-tuple-element.38) | copy-start | bytes 12292
  59.5 20.4 %slice-start.1 = ((f32[8,32,32]{2,1,0:T(8,128)}), f32[1,32,32]{2,1,0:T(8,128)S(1)}, s32[]{:S(2)}) async-start(f32[8,32,32]{2,1,0:T(8,128)} %copy-done.11), calls=%async_computation.1 | async-start | bytes 32768 | tf_op jit(solution)/shard_map/slice | solution.py:161
  59.6 30.7 %copy-start.20 = (bf16[1,1024,32]{1,2,0:T(8,128)(2,1)S(1)}, bf16[1,1024,32]{1,2,0:T(8,128)(2,1)}, u32[]{:S(2)}) copy-start(bf16[1,1024,32]{1,2,0:T(8,128)(2,1)} %param.28) | copy-start | bytes 196612
  61.8 27.9 %collective-permute-start.3 = (bf16[1,128,160]{1,2,0:T(8,128)(2,1)S(1)}, bf16[1,128,160]{1,2,0:T(8,128)(2,1)S(1)}, u32[]{:S(2)}, u32[]{:S(2)}) collective-permute-start(bf16[1,128,160]{1,2,0:T(8,128)(2,1)S(1)} %bitcast.412), channel_id=1, source_target_pairs={{1,0},{2,1},{3,2},{4,3},{5,4},{6,5},{7,6},{8,7},{9,8},{10,9},{11,1... | collective-permute-start | bytes 122888 | tf_op jit(solution)/shard_map/ppermute | solution.py:17
  65.9 23.7 %collective-permute-start.2 = (bf16[1,128,160]{1,2,0:T(8,128)(2,1)S(1)}, bf16[1,128,160]{1,2,0:T(8,128)(2,1)S(1)}, u32[]{:S(2)}, u32[]{:S(2)}) collective-permute-start(bf16[1,128,160]{1,2,0:T(8,128)(2,1)S(1)} %bitcast.413), channel_id=1, source_target_pairs={{0,1},{1,2},{2,3},{3,4},{4,5},{5,6},{6,7},{7,8},{8,9},{9,10},{10,1... | collective-permute-start | bytes 122888 | tf_op jit(solution)/shard_map/ppermute | solution.py:15
  90.3 13.0 %copy-start.18 = (f32[4,1,32,32]{2,3,1,0:T(8,128)S(1)}, f32[4,1,32,32]{2,3,1,0:T(8,128)}, u32[]{:S(2)}) copy-start(f32[4,1,32,32]{2,3,1,0:T(8,128)} %custom-call.48) | copy-start | bytes 49156
  90.3 13.1 %copy-start.19 = (f32[4,32,32]{2,1,0:T(8,128)S(1)}, f32[4,32,32]{2,1,0:T(8,128)}, u32[]{:S(2)}) copy-start(f32[4,32,32]{2,1,0:T(8,128)} %copy.187) | copy-start | bytes 49156
  104.5 7.3 %copy-start.25 = (pred[32,32]{1,0:T(8,128)(4,1)S(1)}, pred[32,32]{1,0:T(8,128)(4,1)}, u32[]{:S(2)}) copy-start(pred[32,32]{1,0:T(8,128)(4,1)} %copy-done.24) | copy-start | bytes 3076
  104.5 7.5 %copy-start.23 = (pred[32,32]{1,0:T(8,128)(4,1)S(1)}, pred[32,32]{1,0:T(8,128)(4,1)}, u32[]{:S(2)}) copy-start(pred[32,32]{1,0:T(8,128)(4,1)} %copy-done.22) | copy-start | bytes 3076
  135.2 33.1 %copy-start.44 = (pred[4]{0:T(512)(128)(4,1)S(1)}, pred[4]{0:T(512)(128)(4,1)}, u32[]{:S(2)}) copy-start(pred[4]{0:T(512)(128)(4,1)} %constant.263.clone.1) | copy-start | bytes 16
  152.4 32.1 %copy-start.17 = (f32[4,32,32]{1,2,0:T(8,128)S(1)}, f32[4,32,32]{1,2,0:T(8,128)}, u32[]{:S(2)}) copy-start(f32[4,32,32]{1,2,0:T(8,128)} %copy.210) | copy-start | bytes 49156
  215.4 4.7 %collective-permute-start.5 = (bf16[1,128,160]{1,2,0:T(8,128)(2,1)S(1)}, bf16[1,128,160]{1,2,0:T(8,128)(2,1)S(1)}, u32[]{:S(2)}, u32[]{:S(2)}) collective-permute-start(bf16[1,128,160]{1,2,0:T(8,128)(2,1)S(1)} %get-tuple-element.34), channel_id=1, source_target_pairs={{1,0},{2,1},{3,2},{4,3},{5,4},{6,5},{7,6},{8,7},{9,8},{10,9},{11,1... | collective-permute-start | bytes 122888 | tf_op jit(solution)/shard_map/ppermute | solution.py:17
  217.3 7.1 %collective-permute-start.4 = (bf16[1,128,160]{1,2,0:T(8,128)(2,1)S(1)}, bf16[1,128,160]{1,2,0:T(8,128)(2,1)S(1)}, u32[]{:S(2)}, u32[]{:S(2)}) collective-permute-start(bf16[1,128,160]{1,2,0:T(8,128)(2,1)S(1)} %get-tuple-element.33), channel_id=1, source_target_pairs={{0,1},{1,2},{2,3},{3,4},{4,5},{5,6},{6,7},{7,8},{8,9},{9,10},{10,1... | collective-permute-start | bytes 122888 | tf_op jit(solution)/shard_map/ppermute | solution.py:15
  228.9 7.1 %copy-start.31 = (s32[1024]{0:T(1024)S(1)}, s32[1024]{0:T(1024)}, u32[]{:S(2)}) copy-start(s32[1024]{0:T(1024)} %copy-done.30) | copy-start | bytes 12292
  231.4 6.9 %collective-permute-start.7 = (bf16[1,128,160]{2,1,0:T(8,128)(2,1)}, bf16[1,128,160]{2,1,0:T(8,128)(2,1)S(1)}, u32[]{:S(2)}, u32[]{:S(2)}) collective-permute-start(bf16[1,128,160]{2,1,0:T(8,128)(2,1)} %bitcast.124), channel_id=1, source_target_pairs={{1,0},{2,1},{3,2},{4,3},{5,4},{6,5},{7,6},{8,7},{9,8},{10,9},{11,1... | collective-permute-start | bytes 122888 | tf_op jit(solution)/shard_map/ppermute | solution.py:17
  233.4 8.3 %collective-permute-start.6 = (bf16[1,128,160]{2,1,0:T(8,128)(2,1)S(1)}, bf16[1,128,160]{2,1,0:T(8,128)(2,1)S(1)}, u32[]{:S(2)}, u32[]{:S(2)}) collective-permute-start(bf16[1,128,160]{2,1,0:T(8,128)(2,1)S(1)} %bitcast.407), channel_id=1, source_target_pairs={{0,1},{1,2},{2,3},{3,4},{4,5},{5,6},{6,7},{7,8},{8,9},{9,10},{10,1... | collective-permute-start | bytes 122888 | tf_op jit(solution)/shard_map/ppermute | solution.py:15
  236.7 4.9 %copy-start.3 = (f32[768,160]{0,1:T(8,128)S(1)}, f32[768,160]{0,1:T(8,128)}, u32[]{:S(2)}) copy-start(f32[768,160]{0,1:T(8,128)} %get-tuple-element.54) | copy-start | bytes 1474564
  241.7 45.2 %copy-start.2 = (f32[768,160]{0,1:T(8,128)S(1)}, f32[768,160]{0,1:T(8,128)}, u32[]{:S(2)}) copy-start(f32[768,160]{0,1:T(8,128)} %param.20) | copy-start | bytes 1474564
  (23 other events, 56.1 us)
where the time goes:
time: 290 us; the launch traced here: 289 us
  blocking collectives  142 us (49%)
  other arithmetic  79.4 us (27%)
  matrix products  21.8 us (8%)
  starting transfers between devices  18.9 us (7%)
  local copies, waits for them, and re-layouts  17.4 us (6%)
  waiting for transfers between devices  7.38 us (3%)
    psum x1, blocking collectives, shards(): inner = lax.psum(jnp.sum(residual_start * owned, axis=0), ('grp', 'sub'))  44.1 us
    another operation x15, other arithmetic, chol_solve(): lax.linalg.triangular_solve(factor, halfway, left_side=True, lower=True,...  34 us
    another operation x15, other arithmetic, solve_chain(): factor = jnp.linalg.cholesky(diag_odd)  31.6 us
    all_gather x1, blocking collectives, shards(): blocks_up = lax.all_gather(coarse_up, 'sub', axis=0, tiled=True)  14.8 us
    all_gather x1, blocking collectives, shards(): blocks_diag = lax.all_gather(coarse_diag, 'sub', axis=0, tiled=True)  14 us
    all_gather x1, blocking collectives, shards(): columns = lax.all_gather(coarse_in[None], 'sub', axis=0, tiled=True)  12.7 us
    ppermute x4, starting transfers between devices, with_halo(): lax.ppermute(head, axis, [((i + 1) % count, i) for i in range(ends)])  9.75 us
    ppermute x4, starting transfers between devices, with_halo(): lax.ppermute(tail, axis, [(i, (i + 1) % count) for i in range(ends)])  9.13 us
  transfers between devices with their start and end apart: 8, of which 2 were waited for; matrix products, arithmetic and copies ran while one was open for 12% of the time, Pallas kernels for 0%

commit v1 on v0

--- a/solution.py
+++ b/solution.py
@@ -188,7 +188,7 @@
     owned = correction[intersection : intersection + rows_own]
     owned = owned.at[sent_right_rows].add(returned[3])
     owned = owned.at[sent_left_rows].add(returned[0])
-    inner = lax.psum(jnp.sum(residual_start * owned, axis=0), ("grp", "sub"))
+    inner = lax.psum(lax.psum(jnp.sum(residual_start * owned, axis=0), "sub"), "grp")
     image = apply_operator(owned)
     curvature = lax.psum(jnp.sum(owned * image, axis=0), ("grp", "sub"))
     step_size = inner / curvature

time: 290 us -> 313 us (1.079)
  blocking collectives: 142 us -> 165 us
    psum x1 -> x3, blocking collectives: 44.1 us -> 66.6 us  [the longest x1 43.5 us: shards(): curvature = lax.psum(jnp.sum(owned * image, axis=0), ('grp', 'sub'))]
  transfers between devices with their start and end apart: 8 -> 8, of which waited for: 2 -> 2; matrix products, arithmetic and copies ran while one was open for 12% -> 11% of each run, Pallas kernels for 0% -> 0%
where the time goes in v1:
time: 313 us; the launch traced here: 312 us
  blocking collectives  165 us (53%)
  other arithmetic  79.4 us (25%)
  matrix products  21.8 us (7%)
  starting transfers between devices  18.9 us (6%)
  local copies, waits for them, and re-layouts  17.5 us (6%)
  waiting for transfers between devices  7.4 us (2%)
    psum x1, blocking collectives, shards(): curvature = lax.psum(jnp.sum(owned * image, axis=0), ('grp', 'sub'))  43.5 us
    another operation x15, other arithmetic, chol_solve(): lax.linalg.triangular_solve(factor, halfway, left_side=True, lower=True,...  34 us
    another operation x15, other arithmetic, solve_chain(): factor = jnp.linalg.cholesky(diag_odd)  31.6 us
    all_gather x1, blocking collectives, shards(): blocks_up = lax.all_gather(coarse_up, 'sub', axis=0, tiled=True)  14.8 us
    all_gather x1, blocking collectives, shards(): blocks_diag = lax.all_gather(coarse_diag, 'sub', axis=0, tiled=True)  14 us
    psum x1, blocking collectives, shards(): lax.psum(jnp.sum(residual_start * owned, axis=0), 'sub')  13.9 us
    all_gather x1, blocking collectives, shards(): columns = lax.all_gather(coarse_in[None], 'sub', axis=0, tiled=True)  12.7 us
    ppermute x4, starting transfers between devices, with_halo(): lax.ppermute(head, axis, [((i + 1) % count, i) for i in range(ends)])  9.75 us
  transfers between devices with their start and end apart: 8, of which 2 were waited for; matrix products, arithmetic and copies ran while one was open for 11% of the time, Pallas kernels for 0%

profile of v1, /device:TPU:14, one launch (start us, length us, event | category | flops | bytes accessed | tf_op | source)
XLA Modules:
  0.0 311.8 jit_solution(4640427087524515887)
XLA Ops:
  10.4 14.8 %all_gather.32 = f32[8,32,32]{2,1,0:T(8,128)S(1)} all-gather(f32[1,32,32]{2,1,0:T(8,128)S(1)} %copy-done.34), channel_id=1, replica_groups=mesh['grp'=4,'sub'=8] {'sub'}, dimensions={0}, use_global_device_ids=true | all-gather | bytes 36864 | tf_op jit(solution)/shard_map/all_gather | solution.py:137
  25.2 14.0 %all_gather.30 = f32[8,32,32]{2,1,0:T(8,128)S(1)} all-gather(f32[1,32,32]{2,1,0:T(8,128)S(1)} %copy-done.35), channel_id=1, replica_groups=mesh['grp'=4,'sub'=8] {'sub'}, dimensions={0}, use_global_device_ids=true | all-gather | bytes 36864 | tf_op jit(solution)/shard_map/all_gather | solution.py:136
  39.5 11.7 %custom-call.47 = f32[4,32,32]{2,1,0:T(8,128)S(1)} custom-call(f32[4,32,32]{2,1,0:T(8,128)S(1)} %copy.185), custom_call_target="Cholesky" | custom-call | tf_op jit(solution)/shard_map/jit(cholesky)/cholesky | solution.py:55
  61.9 4.0 %collective-permute-start.3 = (bf16[1,128,160]{1,2,0:T(8,128)(2,1)S(1)}, bf16[1,128,160]{1,2,0:T(8,128)(2,1)S(1)}, u32[]{:S(2)}, u32[]{:S(2)}) collective-permute-start(bf16[1,128,160]{1,2,0:T(8,128)(2,1)S(1)} %bitcast.412), channel_id=1, source_target_pairs={{1,0},{2,1},{3,2},{4,3},{5,4},{6,5},{7,6},{8,7},{9,8},{10,9},{11,1... | collective-permute-start | bytes 122888 | tf_op jit(solution)/shard_map/ppermute | solution.py:17
  68.7 11.2 %custom-call.48 = f32[4,1,32,32]{2,3,1,0:T(8,128)} custom-call(f32[4,1,32,32]{3,2,1,0:T(8,128)} %select_bitcast_fusion), custom_call_target="InvertDiagBlocksLowerTriangular" | custom-call | tf_op jit(solution)/shard_map/triangular_solve | solution.py:26
  79.9 9.1 %all_gather.31 = f32[4,32,32]{2,1,0:T(8,128)S(1)} all-gather(f32[1,32,32]{2,1,0:T(8,128)S(1)} %slice-done.1), channel_id=1, replica_groups=mesh['grp'=4,'sub'=8] {'grp'}, dimensions={0}, use_global_device_ids=true | all-gather | bytes 20480 | tf_op jit(solution)/shard_map/all_gather | solution.py:161
  90.6 12.7 %all-gather = f32[256,160]{1,0:T(8,128)S(1)} all-gather(f32[32,160]{1,0:T(8,128)S(1)} %convolution_bitcast_fusion.11), channel_id=2, replica_groups=mesh['grp'=4,'sub'=8] {'sub'}, dimensions={0}, use_global_device_ids=true | all-gather | bytes 184320 | tf_op jit(solution)/shard_map/all_gather | solution.py:145
  106.1 5.9 %custom-call.57 = f32[2,32,32]{2,1,0:T(8,128)S(1)} custom-call(f32[2,32,32]{2,1,0:T(8,128)S(1)} %fusion.117), custom_call_target="Cholesky" | custom-call | tf_op jit(solution)/shard_map/jit(cholesky)/cholesky | solution.py:55
  112.2 4.9 %custom-call.49 = f32[2,1,32,32]{2,3,1,0:T(8,128)S(1)} custom-call(f32[2,1,32,32]{3,2,1,0:T(8,128)S(1)} %fusion.119), custom_call_target="InvertDiagBlocksLowerTriangular" | custom-call | tf_op jit(solution)/shard_map/triangular_solve | solution.py:26
  119.2 2.9 custom-call.58
  123.3 2.4 custom-call.50
  127.0 2.9 cholesky.184
  131.1 2.4 custom-call.51
  136.5 7.0 %all-gather.6 = f32[128,160]{1,0:T(8,128)S(1)} all-gather(f32[32,160]{1,0:T(8,128)S(1)} %slice-done), channel_id=8, replica_groups=mesh['grp'=4,'sub'=8] {'grp'}, dimensions={0}, use_global_device_ids=true | all-gather | bytes 102400 | tf_op jit(solution)/shard_map/all_gather | solution.py:162
  143.5 8.9 %all-gather.4 = f32[128,160]{1,0:T(8,128)S(1)} all-gather(f32[32,160]{1,0:T(8,128)S(1)} %convolution_bitcast_fusion.7), channel_id=6, replica_groups=mesh['grp'=4,'sub'=8] {'grp'}, dimensions={0}, use_global_device_ids=true | all-gather | bytes 102400 | tf_op jit(solution)/shard_map/all_gather | solution.py:166
  152.5 7.1 %all-gather.5 = f32[128,160]{1,0:T(8,128)S(1)} all-gather(f32[32,160]{1,0:T(8,128)S(1)} %fusion.101), channel_id=7, replica_groups=mesh['grp'=4,'sub'=8] {'grp'}, dimensions={0}, use_global_device_ids=true | all-gather | bytes 102400 | tf_op jit(solution)/shard_map/all_gather | solution.py:167
  159.7 8.7 %all-gather.3 = f32[128,32]{1,0:T(8,128)S(1)} all-gather(f32[32,32]{1,0:T(8,128)S(1)} %copy.214), channel_id=5, replica_groups=mesh['grp'=4,'sub'=8] {'grp'}, dimensions={0}, use_global_device_ids=true | all-gather | bytes 20480 | tf_op jit(solution)/shard_map/all_gather | solution.py:165
  168.6 6.7 %all-gather.2 = f32[128,32]{1,0:T(8,128)S(1)} all-gather(f32[32,32]{1,0:T(8,128)S(1)} %fusion.145), channel_id=4, replica_groups=mesh['grp'=4,'sub'=8] {'grp'}, dimensions={0}, use_global_device_ids=true | all-gather | bytes 20480 | tf_op jit(solution)/shard_map/all_gather | solution.py:164
  175.5 8.9 %all-gather.1 = f32[128,32]{1,0:T(8,128)S(1)} all-gather(f32[32,32]{1,0:T(8,128)S(1)} %copy.208), channel_id=3, replica_groups=mesh['grp'=4,'sub'=8] {'grp'}, dimensions={0}, use_global_device_ids=true | all-gather | bytes 20480 | tf_op jit(solution)/shard_map/all_gather | solution.py:163
  184.7 5.9 %custom-call.59 = f32[2,32,32]{2,1,0:T(8,128)S(1)} custom-call(f32[2,32,32]{2,1,0:T(8,128)S(1)} %fusion.112), custom_call_target="Cholesky" | custom-call | tf_op jit(solution)/shard_map/jit(cholesky)/cholesky | solution.py:55
  190.8 4.9 %custom-call.52 = f32[2,1,32,32]{2,3,1,0:T(8,128)S(1)} custom-call(f32[2,1,32,32]{3,2,1,0:T(8,128)S(1)} %fusion.118), custom_call_target="InvertDiagBlocksLowerTriangular" | custom-call | tf_op jit(solution)/shard_map/triangular_solve | solution.py:26
  197.7 2.9 custom-call.60
  202.0 2.4 custom-call.53
  205.6 2.9 cholesky.216
  209.9 2.4 custom-call.54
  217.4 2.4 collective-permute-start.4
  220.1 4.3 %collective-permute-done.4 = bf16[1,128,160]{1,2,0:T(8,128)(2,1)S(1)} collective-permute-done((bf16[1,128,160]{1,2,0:T(8,128)(2,1)S(1)}, bf16[1,128,160]{1,2,0:T(8,128)(2,1)S(1)}, u32[]{:S(2)}, u32[]{:S(2)}) %collective-permute-start.4) | collective-permute-done | bytes 40992 | tf_op jit(solution)/shard_map/ppermute | solution.py:15
  233.5 2.4 collective-permute-start.6
  238.7 3.1 collective-permute-done.6
  242.9 13.9 %psum.21 = f32[160]{0:T(256)S(1)} all-reduce(f32[160]{0:T(256)S(1)} %get-tuple-element.30), channel_id=1, replica_groups=mesh['grp'=4,'sub'=8] {'sub'}, use_global_device_ids=true, to_apply=%region_11.15 | all-reduce | flops 160 | bytes 1280 | tf_op jit(solution)/shard_map/psum | solution.py:191
  256.8 9.3 %psum.22 = f32[160]{0:T(256)S(1)} all-reduce(f32[160]{0:T(256)S(1)} %psum.21), channel_id=1, replica_groups=mesh['grp'=4,'sub'=8] {'grp'}, use_global_device_ids=true, to_apply=%region_12.16 | all-reduce | flops 160 | bytes 1280 | tf_op jit(solution)/shard_map/psum | solution.py:191
  266.0 43.5 %psum.23 = f32[160]{0:T(256)S(1)} all-reduce(f32[160]{0:T(256)S(1)} %get-tuple-element.29), channel_id=1, replica_groups=mesh['grp'=4,'sub'=8] {'grp','sub'}, use_global_device_ids=true, to_apply=%region_14.18 | all-reduce | flops 160 | bytes 1280 | tf_op jit(solution)/shard_map/psum | solution.py:193
  (284 shorter events, 62.9 us)
Async XLA Ops:
  0.6 213.9 %copy-start = (bf16[1,1024,1024]{2,1,0:T(8,128)(2,1)S(1)}, bf16[1,1024,1024]{2,1,0:T(8,128)(2,1)}, u32[]{:S(2)}) copy-start(bf16[1,1024,1024]{2,1,0:T(8,128)(2,1)} %param.27) | copy-start | bytes 6291460
  0.6 9.5 %copy-start.43 = (s32[1,6,3]{1,0,2:T(1,128)S(1)}, s32[1,6,3]{1,0,2:T(1,128)}, u32[]{:S(2)}) copy-start(s32[1,6,3]{1,0,2:T(1,128)} %param.23) | copy-start | bytes 220
  0.7 9.7 %copy-start.34 = (f32[1,32,32]{2,1,0:T(8,128)S(1)}, f32[1,32,32]{2,1,0:T(8,128)}, u32[]{:S(2)}) copy-start(f32[1,32,32]{2,1,0:T(8,128)} %param.30) | copy-start | bytes 12292
  0.7 24.5 %copy-start.35 = (f32[1,32,32]{2,1,0:T(8,128)S(1)}, f32[1,32,32]{2,1,0:T(8,128)}, u32[]{:S(2)}) copy-start(f32[1,32,32]{2,1,0:T(8,128)} %param.29) | copy-start | bytes 12292
  2.8 7.3 %copy-start.38 = (s32[128]{0:T(128)}, s32[128]{0:T(128)S(1)}, u32[]{:S(2)}) copy-start(s32[128]{0:T(128)S(1)} %get-tuple-element.50) | copy-start | bytes 1540
  2.8 22.4 %copy-start.40 = (s32[128]{0:T(128)}, s32[128]{0:T(128)S(1)}, u32[]{:S(2)}) copy-start(s32[128]{0:T(128)S(1)} %get-tuple-element.49) | copy-start | bytes 1540
  2.8 22.4 %copy-start.36 = (s32[1024]{0:T(1024)}, s32[1024]{0:T(1024)S(1)}, u32[]{:S(2)}) copy-start(s32[1024]{0:T(1024)S(1)} %get-tuple-element.57) | copy-start | bytes 12292
  2.8 22.4 %copy-start.37 = (s32[1024]{0:T(1024)}, s32[1024]{0:T(1024)S(1)}, u32[]{:S(2)}) copy-start(s32[1024]{0:T(1024)S(1)} %get-tuple-element.56) | copy-start | bytes 12292
  4.3 52.1 %collective-permute-start.1 = (bf16[1,128,160]{2,1,0:T(8,128)(2,1)}, bf16[1,128,160]{2,1,0:T(8,128)(2,1)}, u32[]{:S(2)}, u32[]{:S(2)}) collective-permute-start(bf16[1,128,160]{2,1,0:T(8,128)(2,1)} %bitcast.13), channel_id=1, source_target_pairs={{1,0},{2,1},{3,2},{4,3},{5,4},{6,5},{7,6},{8,7},{9,8},{10,9},{11,1... | collective-permute-start | bytes 122888 | tf_op jit(solution)/shard_map/ppermute | solution.py:17
  7.7 49.9 %collective-permute-start = (bf16[1,128,160]{2,1,0:T(8,128)(2,1)}, bf16[1,128,160]{2,1,0:T(8,128)(2,1)}, u32[]{:S(2)}, u32[]{:S(2)}) collective-permute-start(bf16[1,128,160]{2,1,0:T(8,128)(2,1)} %bitcast.9), channel_id=1, source_target_pairs={{0,1},{1,2},{2,3},{3,4},{4,5},{5,6},{6,7},{7,8},{8,9},{9,10},{10,1... | collective-permute-start | bytes 122888 | tf_op jit(solution)/shard_map/ppermute | solution.py:15
  10.1 43.6 %copy-start.24 = (pred[32,32]{1,0:T(8,128)(4,1)}, pred[32,32]{1,0:T(8,128)(4,1)S(1)}, u32[]{:S(2)}) copy-start(pred[32,32]{1,0:T(8,128)(4,1)S(1)} %iota_compare_fusion.3) | copy-start | bytes 3076
  10.2 45.5 %copy-start.22 = (pred[32,32]{1,0:T(8,128)(4,1)}, pred[32,32]{1,0:T(8,128)(4,1)S(1)}, u32[]{:S(2)}) copy-start(pred[32,32]{1,0:T(8,128)(4,1)S(1)} %iota_compare_fusion.7) | copy-start | bytes 3076
  10.4 43.3 %copy-start.30 = (s32[1024]{0:T(1024)}, s32[1024]{0:T(1024)S(1)}, u32[]{:S(2)}) copy-start(s32[1024]{0:T(1024)S(1)} %pad_clamp_fusion.2) | copy-start | bytes 12292
  39.2 12.8 %copy-start.11 = (f32[8,32,32]{2,1,0:T(8,128)}, f32[8,32,32]{2,1,0:T(8,128)S(1)}, u32[]{:S(2)}) copy-start(f32[8,32,32]{2,1,0:T(8,128)S(1)} %all_gather.30) | copy-start | bytes 98308
  56.4 46.9 %copy-start.13 = (f32[1,32,32]{2,1,0:T(8,128)}, f32[1,32,32]{2,1,0:T(8,128)S(1)}, u32[]{:S(2)}) copy-start(f32[1,32,32]{2,1,0:T(8,128)S(1)} %get-tuple-element.36) | copy-start | bytes 12292
  59.5 20.4 %slice-start.1 = ((f32[8,32,32]{2,1,0:T(8,128)}), f32[1,32,32]{2,1,0:T(8,128)S(1)}, s32[]{:S(2)}) async-start(f32[8,32,32]{2,1,0:T(8,128)} %copy-done.11), calls=%async_computation.1 | async-start | bytes 32768 | tf_op jit(solution)/shard_map/slice | solution.py:161
  59.7 30.7 %copy-start.20 = (bf16[1,1024,32]{1,2,0:T(8,128)(2,1)S(1)}, bf16[1,1024,32]{1,2,0:T(8,128)(2,1)}, u32[]{:S(2)}) copy-start(bf16[1,1024,32]{1,2,0:T(8,128)(2,1)} %param.28) | copy-start | bytes 196612
  61.9 27.9 %collective-permute-start.3 = (bf16[1,128,160]{1,2,0:T(8,128)(2,1)S(1)}, bf16[1,128,160]{1,2,0:T(8,128)(2,1)S(1)}, u32[]{:S(2)}, u32[]{:S(2)}) collective-permute-start(bf16[1,128,160]{1,2,0:T(8,128)(2,1)S(1)} %bitcast.412), channel_id=1, source_target_pairs={{1,0},{2,1},{3,2},{4,3},{5,4},{6,5},{7,6},{8,7},{9,8},{10,9},{11,1... | collective-permute-start | bytes 122888 | tf_op jit(solution)/shard_map/ppermute | solution.py:17
  66.0 23.8 %collective-permute-start.2 = (bf16[1,128,160]{1,2,0:T(8,128)(2,1)S(1)}, bf16[1,128,160]{1,2,0:T(8,128)(2,1)S(1)}, u32[]{:S(2)}, u32[]{:S(2)}) collective-permute-start(bf16[1,128,160]{1,2,0:T(8,128)(2,1)S(1)} %bitcast.413), channel_id=1, source_target_pairs={{0,1},{1,2},{2,3},{3,4},{4,5},{5,6},{6,7},{7,8},{8,9},{9,10},{10,1... | collective-permute-start | bytes 122888 | tf_op jit(solution)/shard_map/ppermute | solution.py:15
  90.4 13.0 %copy-start.18 = (f32[4,1,32,32]{2,3,1,0:T(8,128)S(1)}, f32[4,1,32,32]{2,3,1,0:T(8,128)}, u32[]{:S(2)}) copy-start(f32[4,1,32,32]{2,3,1,0:T(8,128)} %custom-call.48) | copy-start | bytes 49156
  90.4 13.1 %copy-start.19 = (f32[4,32,32]{2,1,0:T(8,128)S(1)}, f32[4,32,32]{2,1,0:T(8,128)}, u32[]{:S(2)}) copy-start(f32[4,32,32]{2,1,0:T(8,128)} %copy.187) | copy-start | bytes 49156
  104.6 7.3 %copy-start.25 = (pred[32,32]{1,0:T(8,128)(4,1)S(1)}, pred[32,32]{1,0:T(8,128)(4,1)}, u32[]{:S(2)}) copy-start(pred[32,32]{1,0:T(8,128)(4,1)} %copy-done.24) | copy-start | bytes 3076
  104.6 7.5 %copy-start.23 = (pred[32,32]{1,0:T(8,128)(4,1)S(1)}, pred[32,32]{1,0:T(8,128)(4,1)}, u32[]{:S(2)}) copy-start(pred[32,32]{1,0:T(8,128)(4,1)} %copy-done.22) | copy-start | bytes 3076
  135.3 33.1 %copy-start.44 = (pred[4]{0:T(512)(128)(4,1)S(1)}, pred[4]{0:T(512)(128)(4,1)}, u32[]{:S(2)}) copy-start(pred[4]{0:T(512)(128)(4,1)} %constant.263.clone.1) | copy-start | bytes 16
  152.5 32.1 %copy-start.17 = (f32[4,32,32]{1,2,0:T(8,128)S(1)}, f32[4,32,32]{1,2,0:T(8,128)}, u32[]{:S(2)}) copy-start(f32[4,32,32]{1,2,0:T(8,128)} %copy.210) | copy-start | bytes 49156
  215.5 4.7 %collective-permute-start.5 = (bf16[1,128,160]{1,2,0:T(8,128)(2,1)S(1)}, bf16[1,128,160]{1,2,0:T(8,128)(2,1)S(1)}, u32[]{:S(2)}, u32[]{:S(2)}) collective-permute-start(bf16[1,128,160]{1,2,0:T(8,128)(2,1)S(1)} %get-tuple-element.32), channel_id=1, source_target_pairs={{1,0},{2,1},{3,2},{4,3},{5,4},{6,5},{7,6},{8,7},{9,8},{10,9},{11,1... | collective-permute-start | bytes 122888 | tf_op jit(solution)/shard_map/ppermute | solution.py:17
  217.4 7.1 %collective-permute-start.4 = (bf16[1,128,160]{1,2,0:T(8,128)(2,1)S(1)}, bf16[1,128,160]{1,2,0:T(8,128)(2,1)S(1)}, u32[]{:S(2)}, u32[]{:S(2)}) collective-permute-start(bf16[1,128,160]{1,2,0:T(8,128)(2,1)S(1)} %get-tuple-element.31), channel_id=1, source_target_pairs={{0,1},{1,2},{2,3},{3,4},{4,5},{5,6},{6,7},{7,8},{8,9},{9,10},{10,1... | collective-permute-start | bytes 122888 | tf_op jit(solution)/shard_map/ppermute | solution.py:15
  229.0 7.1 %copy-start.31 = (s32[1024]{0:T(1024)S(1)}, s32[1024]{0:T(1024)}, u32[]{:S(2)}) copy-start(s32[1024]{0:T(1024)} %copy-done.30) | copy-start | bytes 12292
  231.5 6.9 %collective-permute-start.7 = (bf16[1,128,160]{2,1,0:T(8,128)(2,1)}, bf16[1,128,160]{2,1,0:T(8,128)(2,1)S(1)}, u32[]{:S(2)}, u32[]{:S(2)}) collective-permute-start(bf16[1,128,160]{2,1,0:T(8,128)(2,1)} %bitcast.124), channel_id=1, source_target_pairs={{1,0},{2,1},{3,2},{4,3},{5,4},{6,5},{7,6},{8,7},{9,8},{10,9},{11,1... | collective-permute-start | bytes 122888 | tf_op jit(solution)/shard_map/ppermute | solution.py:17
  233.5 8.3 %collective-permute-start.6 = (bf16[1,128,160]{2,1,0:T(8,128)(2,1)S(1)}, bf16[1,128,160]{2,1,0:T(8,128)(2,1)S(1)}, u32[]{:S(2)}, u32[]{:S(2)}) collective-permute-start(bf16[1,128,160]{2,1,0:T(8,128)(2,1)S(1)} %bitcast.407), channel_id=1, source_target_pairs={{0,1},{1,2},{2,3},{3,4},{4,5},{5,6},{6,7},{7,8},{8,9},{9,10},{10,1... | collective-permute-start | bytes 122888 | tf_op jit(solution)/shard_map/ppermute | solution.py:15
  236.8 4.9 %copy-start.3 = (f32[768,160]{0,1:T(8,128)S(1)}, f32[768,160]{0,1:T(8,128)}, u32[]{:S(2)}) copy-start(f32[768,160]{0,1:T(8,128)} %get-tuple-element.52) | copy-start | bytes 1474564
  241.8 67.8 %copy-start.2 = (f32[768,160]{0,1:T(8,128)S(1)}, f32[768,160]{0,1:T(8,128)}, u32[]{:S(2)}) copy-start(f32[768,160]{0,1:T(8,128)} %param.20) | copy-start | bytes 1474564
  (23 other events, 56.2 us)
